TPU v7x, 768 devices: a whole 4x8x12 slice. The times are simulated.
768 devices in a mesh: row: 12 (over z), col: 64 (over x, y, core).
Axes of the slice: x: 4, y: 8, z: 12, core: 2. Of those that a mesh axis runs over, the one named last changes fastest.
Arguments:
- user_factors: bfloat16 [24576, 128], P(('row', 'col')), may hold values from -1.796875 to 1.796875
- item_factors: bfloat16 [64, 768, 128], P('col', 'row'), may hold values from -1.796875 to 1.796875
- ratings: bfloat16 [12, 64, 36, 128, 128], P('row', 'col'), may hold values from 0 to 8, as said below
- tile_cell: int32 [12, 64, 36], P('row', 'col'), may hold values from 0 to 95, as said below
- keep_count: int32 [12, 64], P('row', 'col'), may hold values from 1 to 24, as said below
- send_count: int32 [12, 64, 12], P('row', 'col'), may hold values from 0 to 2, as said below
- user_nbrs: int32 [24576, 16], P(('row', 'col')), may hold values from 0 to 2047
- item_nbrs: int32 [64, 768, 16], P('col', 'row'), may hold values from 0 to 767
Outputs:
- grad_users: float32 [24576, 128], P(('row', 'col'))
- grad_items: float32 [64, 768, 128], P('col', 'row')
Inputs may be any that keep to these rules, and one draw needn't show every extreme that they name: `ratings`: zero marks an unobserved entry; a nonzero value is at least 0.25. `tile_cell`: cells are distinct within a device; cell a * 6 + b is user subtile a of the device's user block and item subtile b of its item block. keep_count plus the sum of send_count is at most 36 on every device and equals 36 on some device of every item block. `send_count`: A device assigns no slots to itself and at most 2 to each other device of its item block; the assigned slots follow its kept slots in the order of the receiving devices; some device assigns exactly 2 to some peer. `user_nbrs`: neighbours index rows of the user's own block. `item_nbrs`: neighbours index rows of the item's own block.
All inputs are finite; a program needn't handle non-finite values.
Results may differ from a plain program's by a relative error of at most 0.0012.
Values may be sent and summed in bfloat16 or wider, within the bound.
A program may use at most 32 MiB of HBM per device.

v0:
```python
import jax
import jax.numpy as jnp
from jax import lax
from jax.sharding import PartitionSpec as P

ALPHA = 0.5
DATA_SCALE = 0.0625
SMOOTH = 4.0


def tile_grads(user_tiles, item_tiles, rating_tiles, weight):
    product = jnp.einsum("gik,gjk->gij", user_tiles, item_tiles, preferred_element_type=jnp.float32)
    values = rating_tiles.astype(jnp.float32)
    prefer = jnp.where(values > 0, 1.0, 0.0).astype(jnp.float32)
    error = (weight[:, None, None] * (1.0 + ALPHA * values) * (product - prefer)).astype(
        jnp.bfloat16
    )
    user_part = jnp.einsum("gij,gjk->gik", error, item_tiles, preferred_element_type=jnp.float32)
    item_part = jnp.einsum("gij,gik->gjk", error, user_tiles, preferred_element_type=jnp.float32)
    return (user_part, item_part)


def place(total, parts, index, count):
    onehot = (index[:, None] == jnp.arange(count)[None, :]).astype(jnp.float32)
    return total + jnp.einsum("ga,gik->aik", onehot, parts, precision=lax.Precision.HIGHEST)


def local_tiles(totals, user_tiles, item_tiles, own_ratings, own_cells, count):
    group_size = 4
    item_count = item_tiles.shape[0]
    user_count = user_tiles.shape[0]

    def step(turn, carry):
        user_acc, item_acc = carry
        start = turn * group_size
        rating_group = lax.dynamic_slice_in_dim(own_ratings, start, group_size, 0)
        cell_group = lax.dynamic_slice_in_dim(own_cells, start, group_size, 0)
        weight = (start + jnp.arange(group_size) < count).astype(jnp.float32)
        upper = cell_group // item_count
        lower = cell_group % item_count
        left = jnp.take(user_tiles, upper, axis=0)
        right = jnp.take(item_tiles, lower, axis=0)
        user_part, item_part = tile_grads(left, right, rating_group, weight)
        return (
            place(user_acc, user_part, upper, user_count),
            place(item_acc, item_part, lower, item_count),
        )

    turns = (count + group_size - 1) // group_size
    return lax.fori_loop(0, turns, step, totals)


def smoothing(own_rows, block, neighbours):
    near = jnp.take(block, neighbours, axis=0).astype(jnp.float32)
    return own_rows.astype(jnp.float32) - jnp.sum(near, axis=1) / neighbours.shape[1]


def local(
    user_factors, item_factors, ratings, tile_cell, keep_count, send_count, user_nbrs, item_nbrs
):
    tile = ratings.shape[-1]
    rank = user_factors.shape[1]
    user_block = lax.all_gather(user_factors, "col", axis=0, tiled=True)
    item_block = lax.all_gather(item_factors[0], "row", axis=0, tiled=True)
    user_tiles = user_block.reshape(-1, tile, rank)
    item_tiles = item_block.reshape(-1, tile, rank)
    user_count = user_tiles.shape[0]
    item_count = item_tiles.shape[0]
    own_ratings = ratings[0, 0]
    own_cells = tile_cell[0, 0]
    keep = keep_count[0, 0]
    sends = send_count[0, 0]
    totals = (
        jnp.zeros((user_count, tile, rank), jnp.float32),
        jnp.zeros((item_count, tile, rank), jnp.float32),
    )
    count = keep + jnp.sum(sends)
    user_acc, item_acc = local_tiles(totals, user_tiles, item_tiles, own_ratings, own_cells, count)
    flat_users = user_acc.reshape(-1, rank)
    flat_items = item_acc.reshape(-1, rank)
    user_rows = user_factors.shape[0]
    item_rows = item_factors.shape[1]
    total_users = lax.psum(flat_users, "col")
    total_items = lax.psum(flat_items, "row")
    share_users = lax.dynamic_slice_in_dim(
        total_users, lax.axis_index("col") * user_rows, user_rows, 0
    )
    share_items = lax.dynamic_slice_in_dim(
        total_items, lax.axis_index("row") * item_rows, item_rows, 0
    )
    user_smooth = smoothing(user_factors, user_block, user_nbrs)
    item_smooth = smoothing(item_factors[0], item_block, item_nbrs[0])
    grad_users = DATA_SCALE * share_users + SMOOTH * user_smooth
    grad_items = DATA_SCALE * share_items + SMOOTH * item_smooth
    return (grad_users, grad_items[None])


def solution(mesh):
    placed = (
        P(("row", "col"), None),
        P("col", "row", None),
        P("row", "col", None, None, None),
        P("row", "col", None),
        P("row", "col"),
        P("row", "col", None),
        P(("row", "col"), None),
        P("col", "row", None),
    )
    return jax.shard_map(
        local,
        mesh=mesh,
        in_specs=placed,
        out_specs=(P(("row", "col"), None), P("col", "row", None)),
        check_vma=False,
    )
```

profile of v0, /device:TPU:1, one launch (start us, length us, event | category | flops | bytes accessed | tf_op | source)
XLA Modules:
  0.0 458.9 jit_solution(14091781783215367669)
XLA Ops:
  7.9 1.3 reduce_sum.27
  9.8 58.0 %all_gather.6 = bf16[2048,128]{1,0:T(8,128)(2,1)S(1)} all-gather(bf16[32,128]{1,0:T(8,128)(2,1)} %param.10), channel_id=1, replica_groups=mesh['row'=12,'col'=64] {'col'}, dimensions={0}, use_global_device_ids=true | all-gather | bytes 532480 | tf_op jit(solution)/shard_map/all_gather | solution.py:63
  67.8 22.7 %all-gather = bf16[1,768,128]{2,1,0:T(8,128)(2,1)S(1)} all-gather(bf16[1,64,128]{2,1,0:T(8,128)(2,1)} %param.11), channel_id=2, replica_groups=mesh['row'=12,'col'=64] {'row'}, dimensions={1}, use_global_device_ids=true | all-gather | bytes 212992 | tf_op jit(solution)/shard_map/all_gather | solution.py:64
  90.6 9.7 %while.14 = (s32[]{:T(128)}, f32[16,128,128]{2,0,1:T(8,128)S(1)}, f32[6,128,128]{2,0,1:T(8,128)S(1)}, s32[]{:T(128)}, s32[36]{0:T(128)S(1)}, /*index=5*/s32[]{:T...) while((s32[]{:T(128)}, f32[16,128,128]{2,0,1:T(8,128)S(1)}, ...), condition=%wide.region_2.3_spmd, body=%wide.region_1.2_spmd.sunk | while | flops 68847840 | bytes 5513667 | solution.py:50
  90.7 0.1 compare_and_fusion.5
  90.8 0.6 gather_fusion
  91.4 0.6 gather_fusion.1
  92.0 1.2 fusion.37
  93.2 0.2 fusion.38
  93.4 1.1 convolution_add_fusion.4
  94.5 0.2 fusion.39
  94.8 0.7 convolution_add_fusion.5
  95.5 0.1 compare_and_fusion.5
  95.7 0.6 gather_fusion
  96.3 0.6 gather_fusion.1
  96.8 1.2 fusion.37
  98.0 0.2 fusion.38
  98.3 1.1 convolution_add_fusion.4
  99.4 0.3 fusion.39
  99.6 0.7 convolution_add_fusion.5
  100.4 0.8 copy.17
  101.3 1.4 copy.14
  103.1 1.3 gather_fusion.2
  104.5 0.1 copy.15
  104.5 0.1 copy.18
  104.7 3.2 gather_fusion.3
  107.9 0.2 convert_reduce_fusion.1
  108.1 0.2 convert_reduce_fusion
  108.3 127.9 %all-reduce.5.cloned.1.call-done = f32[768,128]{1,0:T(8,128)} async-done(((f32[768,128]{1,0:T(8,128)}), f32[768,128]{1,0:T(8,128)}) %all-reduce.5.cloned.1.call-update) | async-done | bytes 393232 | tf_op jit(solution)/shard_map/psum | solution.py:84
  236.2 1.4 fusion.19
  237.6 213.1 %all-reduce.3.cloned.1.call-done = f32[2048,128]{1,0:T(8,128)} async-done(((f32[2048,128]{1,0:T(8,128)}), f32[2048,128]{1,0:T(8,128)}) %all-reduce.3.cloned.1.call-update) | async-done | bytes 1048592 | tf_op jit(solution)/shard_map/psum | solution.py:83
  450.7 1.3 multiply_add_fusion
  (34 shorter events, 0.6 us)
Async XLA Ops:
  7.2 229.0 %all-reduce.5.cloned.1.call-start = ((), (), s32[]{:S(2)}) async-start(), calls=%async_computation.1 | async-start | bytes 786432 | tf_op jit(solution)/shard_map/psum | solution.py:84
  9.8 80.8 %copy-start.4 = (s32[1,1,36]{2,1,0:T(1,128)S(1)}, s32[1,1,36]{2,1,0:T(1,128)}, u32[]{:S(2)}) copy-start(s32[1,1,36]{2,1,0:T(1,128)} %param.13) | copy-start | bytes 436
  101.2 349.5 %all-reduce.3.cloned.1.call-start = ((), (), s32[]{:S(2)}) async-start(), calls=%async_computation | async-start | bytes 2097152 | tf_op jit(solution)/shard_map/psum | solution.py:83
  101.3 1.4 copy-start.2
  101.3 1.4 copy-start.3
  104.7 131.5 %copy-start = (bf16[1,64,128]{2,1,0:T(8,128)(2,1)S(1)}, bf16[1,64,128]{2,1,0:T(8,128)(2,1)}, u32[]{:S(2)}) copy-start(bf16[1,64,128]{2,1,0:T(8,128)(2,1)} %param.11) | copy-start | bytes 49156
  104.7 346.0 %copy-start.1 = (bf16[32,128]{1,0:T(8,128)(2,1)S(1)}, bf16[32,128]{1,0:T(8,128)(2,1)}, u32[]{:S(2)}) copy-start(bf16[32,128]{1,0:T(8,128)(2,1)} %param.10) | copy-start | bytes 24580
Sparse Core Ops, SparseCore 0:
  101.4 134.7 all-reduce.4
  240.0 210.6 all-reduce.2
where the time goes:
time: 459 us
  waiting for transfers between devices  341 us (74%)
  blocking collectives  80.7 us (18%)
  between operations  15.5 us (3%)
  local copies, waits for them, and re-layouts  9.65 us (2%)
  matrix products  7.01 us (2%)
  other arithmetic  4.66 us (1%)
    psum x1, waiting for transfers between devices, local(): total_users = lax.psum(flat_users, 'col')  213 us
    psum x1, waiting for transfers between devices, local(): total_items = lax.psum(flat_items, 'row')  128 us
    all_gather x1, blocking collectives, local(): user_block = lax.all_gather(user_factors, 'col', axis=0, tiled=True)  58 us
    all_gather x1, blocking collectives, local(): item_block = lax.all_gather(item_factors[0], 'row', axis=0, tiled=True)  22.7 us
  transfers between devices with their start and end apart: 2, of which 2 were waited for; matrix products, arithmetic and copies ran while one was open for 2% of the time, Pallas kernels for 0%

commit v1 on v0

v1 whole, which is shorter than its diff:
```python
import functools

import jax
import jax.numpy as jnp
from jax import lax
from jax.experimental import pallas as pl
from jax.experimental.pallas import tpu as pltpu
from jax.sharding import PartitionSpec as P

ALPHA = 0.5
DATA_SCALE = 0.0625
SMOOTH = 4.0

NX, NY, NC = 4, 8, 2
CHIPS = NX * NY
MESH = pl.DeviceIdType.MESH
F32 = jnp.float32
BF16 = jnp.bfloat16


def ring_order(n):
    order = []
    for d in range(1, n // 2 + 1):
        order.append(d)
        if d != n - d:
            order.append(n - d)
    return order


def neighbour_counts(nbrs, width):
    nbrs = jnp.transpose(nbrs)
    rows, knn = nbrs.shape
    place = lax.broadcasted_iota(jnp.int32, (rows, width), 1)
    total = jnp.zeros((rows, width), F32)
    for k in range(knn):
        total = total + jnp.where(nbrs[:, k : k + 1] == place, 1.0, 0.0)
    return total.astype(BF16)


def kernel(
    nrow, lag,
    uf, vf, ratings, cells, keep, sends, unbr, vnbr,
    gu, gi,
    ug, vg, rat, er, ua, it, itf, pr, us, ur, ist, ir, au, ai, invv, invs,
    y_recv, x_recv, p_recv, z_recv, pr_recv, ur_recv, ir_recv,
    y_send, x_send, p_send, z_send, pr_send, ur_send, ir_send, loc_sem, inv_sem,
):
    r = lax.axis_index("row")
    col = lax.axis_index("col")
    c = lax.rem(col, NC)
    other = 1 - c
    p = col // NC
    x = p // NY
    y = lax.rem(p, NY)
    slots, tile = ratings.shape[2], ratings.shape[3]
    vt = nrow * vf.shape[1] // tile
    steps = CHIPS // 4
    urows = uf.shape[0]
    irows = vf.shape[1]

    def dev(chip, core):
        return (r, chip * NC + core)

    def remote(src, dst, ssem, rsem, device):
        return pltpu.make_async_remote_copy(
            src_ref=src, dst_ref=dst, send_sem=ssem, recv_sem=rsem,
            device_id=device, device_id_type=MESH,
        )

    load = pltpu.make_async_copy(ratings.at[0, 0], rat, loc_sem)
    load.start()

    barrier = pltpu.get_barrier_semaphore()

    def greet_plane(d, _):
        chip = lax.rem(p + d, CHIPS)
        pl.semaphore_signal(barrier, inc=1, device_id=dev(chip, c), device_id_type=MESH)
        return 0

    def greet_z(d, _):
        pl.semaphore_signal(barrier, inc=1, device_id=(lax.rem(r + d, nrow), col), device_id_type=MESH)
        return 0

    lax.fori_loop(1, nrow, greet_z, 0)
    lax.fori_loop(1, CHIPS, greet_plane, 0)
    pl.semaphore_signal(barrier, inc=1, device_id=dev(p, other), device_id_type=MESH)

    live = keep[0, 0]
    for q in range(nrow):
        live = live + sends[0, 0, q]
    slot_at = lax.broadcasted_iota(jnp.int32, (128, slots), 1)
    cell_at = lax.broadcasted_iota(jnp.int32, (128, slots), 0)
    held = jnp.where((cells[0] == cell_at) & (slot_at < live), slot_at + 1, 0)
    by_cell = jnp.sum(held.astype(F32), axis=1, keepdims=True)
    wide = jnp.transpose(jnp.broadcast_to(by_cell, (128, 128)))
    invv[...] = wide[0:8, :].astype(jnp.int32)
    inv_copy = pltpu.make_async_copy(invv, invs, inv_sem)
    inv_copy.start()

    au[...] = neighbour_counts(unbr[...], au.shape[1])
    ai[...] = neighbour_counts(vnbr[0], ai.shape[1])
    ug[p, c] = uf[...]
    vg[r] = vf[0]
    ur[p] = jnp.zeros(ur.shape[1:], BF16)
    ir[r] = jnp.zeros(ir.shape[1:], BF16)
    it[...] = jnp.zeros_like(it)

    pl.semaphore_wait(barrier, nrow - 1 + CHIPS - 1 + 1)

    def send_z(d, _):
        to = lax.rem(r + d, nrow)
        remote(vf.at[0], vg.at[r], z_send, z_recv, (to, col)).start()
        return 0

    def send_y(d, _):
        chip = x * NY + lax.rem(y + d, NY)
        remote(uf, ug.at[p, c], y_send, y_recv.at[y], dev(chip, c)).start()
        return 0

    def spread_x(src, chip):
        def one(d, _):
            to = lax.rem(x + d, NX) * NY + y
            remote(src, ug.at[chip, c], x_send, x_recv.at[chip], dev(to, c)).start()
            return 0

        lax.fori_loop(1, NX, one, 0)

    def to_partner(src, chip):
        remote(src, ug.at[chip, c], p_send, p_recv, dev(p, other)).start()

    lax.fori_loop(1, NY, send_y, 0)
    lax.fori_loop(1, nrow, send_z, 0)
    spread_x(uf, p)
    to_partner(uf, p)

    for d in ring_order(NY):
        yy = lax.rem(y + d, NY)
        chip = x * NY + yy
        piece = ug.at[chip, c]
        remote(piece, piece, y_send, y_recv.at[yy], dev(p, other)).wait_recv()
        spread_x(piece, chip)
        to_partner(piece, chip)
    for d in [0] + ring_order(NY):
        yy = lax.rem(y + d, NY)
        for dx in ring_order(NX):
            chip = lax.rem(x + dx, NX) * NY + yy
            piece = ug.at[chip, c]
            remote(piece, piece, x_send, x_recv.at[chip], dev(p, other)).wait_recv()
            to_partner(piece, chip)

    inv_copy.wait()
    load.wait()
    some = vg.at[pl.ds(0, nrow - 1)]
    remote(some, some, z_send, z_recv, dev(p, other)).wait_recv()
    some = ug.at[:, other]
    remote(some, some, p_send, p_recv, dev(p, other)).wait_recv()

    first = p // 4 + 1

    def pass_on(i):
        t = lax.rem(first + i + steps, steps)
        four = pl.ds(t * 4, 4)
        remote(pr.at[four], pr.at[four], pr_send, pr_recv.at[t], dev(p, other)).wait_recv()
        us[four] = (ua[four, c] + pr[four]).astype(BF16)

        def one(j, _):
            chip = t * 4 + j

            @pl.when(chip != p)
            def _():
                remote(us.at[chip], ur.at[p], ur_send, ur_recv, dev(chip, c)).start()

            return 0

        lax.fori_loop(0, 4, one, 0)

    def step(i, _):
        t = lax.rem(first + i, steps)
        four = pl.ds(t * 4, 4)
        users = ug[four].reshape(2 * tile, -1)
        for pair in range(vt // 2):
            items = vg[pl.ds(pair * (2 * tile // irows), 2 * tile // irows)].reshape(2 * tile, -1)
            product = lax.dot_general(
                users, items, (((1,), (1,)), ((), ())), preferred_element_type=F32
            )
            for a in range(2):
                for b in range(2):
                    slot = invs[0, (t * 2 + a) * vt + pair * 2 + b]
                    weight = jnp.minimum(slot, 1).astype(F32)
                    values = rat[jnp.clip(slot - 1, 0, slots - 1)].astype(F32)
                    prefer = jnp.where(values > 0, 1.0, 0.0).astype(F32)
                    part = product[a * tile : (a + 1) * tile, b * tile : (b + 1) * tile]
                    error = (weight + (ALPHA * weight) * values) * (part - prefer)
                    er[a * tile : (a + 1) * tile, (pair * 2 + b) * tile : (pair * 2 + b + 1) * tile] = error.astype(BF16)
        error = er[...]
        items = vg[...].reshape(vt * tile, -1)
        user_part = jnp.dot(error, items, preferred_element_type=F32)
        ua[four] = user_part.reshape(4, NC, urows, -1)
        it[...] += lax.dot_general(users, error, (((0,), (0,)), ((), ())), preferred_element_type=F32)
        remote(ua.at[four, other], pr.at[four], pr_send, pr_recv.at[t], dev(p, other)).start()

        @pl.when(i >= lag)
        def _():
            pass_on(i - lag)

        return 0

    lax.fori_loop(0, steps, step, 0)

    item_total = jnp.transpose(it[...]).reshape(nrow, irows, -1)
    itf[...] = item_total
    ist[...] = item_total.astype(BF16)

    def send_items(d, _):
        to = lax.rem(r + d, nrow)
        remote(ist.at[to], ir.at[r], ir_send, ir_recv, (to, col)).start()
        return 0

    lax.fori_loop(1, nrow, send_items, 0)
    for i in range(steps - lag, steps):
        pass_on(i)

    near = jnp.dot(au[...], ug[...].reshape(CHIPS * NC * urows, -1), preferred_element_type=F32)
    user_smooth = uf[...].astype(F32) - near / unbr.shape[0]
    near = jnp.dot(ai[...], vg[...].reshape(vt * tile, -1), preferred_element_type=F32)
    item_smooth = vf[0].astype(F32) - near / vnbr.shape[1]

    some = ur.at[pl.ds(0, CHIPS - 1)]
    remote(some, some, ur_send, ur_recv, dev(p, other)).wait_recv()
    total = ua[p, c] + pr[p] + jnp.sum(ur[...].astype(F32), axis=0)
    gu[...] = DATA_SCALE * total + SMOOTH * user_smooth
    some = ir.at[pl.ds(0, nrow - 1)]
    remote(some, some, ir_send, ir_recv, dev(p, other)).wait_recv()
    total = itf[r] + jnp.sum(ir[...].astype(F32), axis=0)
    gi[0] = DATA_SCALE * total + SMOOTH * item_smooth

    def left(view, sem):
        remote(view, view, sem, ur_recv, dev(p, other)).wait_send()

    left(ug.at[pl.ds(0, NY - 1), c], y_send)
    left(ug.at[pl.ds(0, (NX - 1) * NY), c], x_send)
    left(ug.at[:, c], p_send)
    left(vg.at[pl.ds(0, nrow - 1)], z_send)
    left(pr, pr_send)
    left(us.at[pl.ds(0, CHIPS - 1)], ur_send)
    left(ist.at[pl.ds(0, nrow - 1)], ir_send)


def finish(u_in, i_in, gu, gi):
    gu[...] = u_in[...]
    gi[...] = i_in[...]


def solution(mesh):
    nrow = mesh.shape["row"]
    placed = (
        P(("row", "col"), None),
        P("col", "row", None),
        P("row", "col", None, None, None),
        P("row", "col", None),
        P("row", "col"),
        P("row", "col", None),
        P(("row", "col"), None),
        P("col", "row", None),
    )

    def local(uf, vf, ratings, cells, keep, sends, unbr, vnbr):
        urows, rank = uf.shape
        irows = vf.shape[1]
        slots, tile = ratings.shape[2], ratings.shape[3]
        outs_shape = (
            jax.ShapeDtypeStruct((urows, rank), F32),
            jax.ShapeDtypeStruct((1, irows, rank), F32),
        )
        vmem = pl.BlockSpec(memory_space=pltpu.VMEM)
        smem = pl.BlockSpec(memory_space=pltpu.SMEM)
        hbm = pl.BlockSpec(memory_space=pl.ANY)
        dma = pltpu.SemaphoreType.DMA
        V = pltpu.VMEM
        outs = pl.pallas_call(
            functools.partial(kernel, nrow, 2),
            out_shape=outs_shape,
            in_specs=[vmem, vmem, hbm, vmem, smem, smem, vmem, vmem],
            out_specs=(vmem, vmem),
            scratch_shapes=[
                V((CHIPS, NC, urows, rank), BF16),
                V((nrow, irows, rank), BF16),
                V((slots, tile, tile), BF16),
                V((2 * tile, nrow * irows), BF16),
                V((CHIPS, NC, urows, rank), F32),
                V((rank, nrow * irows), F32),
                V((nrow, irows, rank), F32),
                V((CHIPS, urows, rank), F32),
                V((CHIPS, urows, rank), BF16),
                V((CHIPS, urows, rank), BF16),
                V((nrow, irows, rank), BF16),
                V((nrow, irows, rank), BF16),
                V((urows, CHIPS * NC * urows), BF16),
                V((irows, nrow * irows), BF16),
                V((8, 128), jnp.int32),
                pltpu.SMEM((8, 128), jnp.int32),
                dma((NY,)), dma((CHIPS,)), dma, dma, dma((CHIPS // 4,)), dma, dma,
                dma, dma, dma, dma, dma, dma, dma, dma, dma,
            ],
            compiler_params=pltpu.CompilerParams(collective_id=0, has_side_effects=True),
        )(uf, vf, ratings, cells, keep, sends, unbr.T, jnp.swapaxes(vnbr, 1, 2))
        return pl.pallas_call(
            finish,
            out_shape=outs_shape,
            in_specs=[vmem, vmem],
            out_specs=(vmem, vmem),
        )(*outs)

    return jax.shard_map(
        local,
        mesh=mesh,
        in_specs=placed,
        out_specs=(P(("row", "col"), None), P("col", "row", None)),
        check_vma=False,
    )
```

time: 459 us -> 49.6 us (0.11)
  waiting for transfers between devices: 341 us -> 0 us
  blocking collectives: 80.7 us -> 0 us
  Pallas kernels: 0 us -> 48 us
  between operations: 15.5 us -> 1.29 us
  local copies, waits for them, and re-layouts: 9.65 us -> 0 us
  matrix products: 7.01 us -> 0 us
  other arithmetic: 4.66 us -> 0 us
    psum x2 -> x0, waiting for transfers between devices: 341 us -> none  [the longest x1 213 us: local(): total_users = lax.psum(flat_users, 'col')]
    all_gather x2 -> x0, blocking collectives: 80.7 us -> none  [the longest x1 58 us: local(): user_block = lax.all_gather(user_factors, 'col', axis=0, tiled=True)]
    pallas_call x0 -> x2, Pallas kernels: none -> 48 us  [the longest x1 46.6 us: local(): pl.pallas_call(functools.partial(kernel, nrow, 2), out_shape=outs_shape,...]
    dot_general x10 -> x0, matrix products: 7.01 us -> none  [the longest x4 3.62 us: place(): jnp.einsum('ga,gik->aik', onehot, parts, precision=lax.Precision.HIGHEST)]
    gather x6 -> x0, local copies, waits for them, and re-layouts: 6.83 us -> none  [the longest x2 4.55 us: smoothing(): near = jnp.take(block, neighbours, axis=0).astype(jnp.float32)]
  transfers between devices with their start and end apart: 2 -> 0, of which waited for: 2 -> 0; matrix products, arithmetic and copies ran while one was open for 2% -> 0% of each run, Pallas kernels for 0% -> 0%
where the time goes in v1:
time: 49.6 us; the launch traced here: 49.3 us
  Pallas kernels  48 us (97%)
  between operations  1.29 us (3%)
    pallas_call x1, Pallas kernels, local(): pl.pallas_call(functools.partial(kernel, nrow, 2), out_shape=outs_shape,...  46.6 us
    pallas_call x1, Pallas kernels, local(): pl.pallas_call(finish, out_shape=outs_shape, in_specs=[vmem, vmem], out_s...  1.4 us

profile of v1, /device:TPU:1, one launch (start us, length us, event | category | flops | bytes accessed | tf_op | source)
XLA Modules:
  0.0 49.3 jit_solution(15920036447446598914)
XLA Ops:
  1.3 46.6 %shard_map.95 = (f32[32,128]{1,0:T(8,128)}, f32[1,64,128]{2,1,0:T(8,128)}) custom-call(bf16[32,128]{1,0:T(8,128)(2,1)} %uf.1, bf16[1,64,128]{2,1,0:T(8,128)(2,1)} %vf.1, bf16[1,1,36,128,128]{4,3,2,1,0:T(8,128)(2,1)} %ratings.1, s32[1,1,36]{2,1,0:T(1,128)} %cells.1, s32[1,1]{1,0:T(1,128)S(6)} %copy.10.keep, s32[1,1,12]{2,1,0:T(1,128)} %sends.1, ...), custom_call_target="tpu_custom_call" | custom-call | tf_op jit(solution)/shard_map/pallas_call | solution.py:280
  47.9 1.4 %shard_map.96 = (f32[32,128]{1,0:T(8,128)}, f32[1,64,128]{2,1,0:T(8,128)}) custom-call(f32[32,128]{1,0:T(8,128)} %get-tuple-element.4.u_in, f32[1,64,128]{2,1,0:T(8,128)} %get-tuple-element.5.i_in), custom_call_target="tpu_custom_call" | custom-call | tf_op jit(solution)/shard_map/pallas_call | solution.py:307

commit v2 on v1

--- a/solution.py
+++ b/solution.py
@@ -25,6 +25,10 @@
         if d != n - d:
             order.append(n - d)
     return order
+
+
+def far_first(n):
+    return ring_order(n)[::-1]
 
 
 def neighbour_counts(nbrs, width):
@@ -39,8 +43,9 @@
 
 def kernel(
     nrow, lag,
-    uf, vf, ratings, cells, keep, sends, unbr, vnbr,
+    uf_hbm, vf_hbm, ratings, cells_hbm, keep_hbm, sends_hbm, unbr_hbm, vnbr_hbm,
     gu, gi,
+    uf, vf, cells, keep, sends, unbr, vnbr,
     ug, vg, rat, er, ua, it, itf, pr, us, ur, ist, ir, au, ai, invv, invs,
     y_recv, x_recv, p_recv, z_recv, pr_recv, ur_recv, ir_recv,
     y_send, x_send, p_send, z_send, pr_send, ur_send, ir_send, loc_sem, inv_sem,
@@ -67,27 +72,39 @@
             device_id=device, device_id_type=MESH,
         )
 
-    load = pltpu.make_async_copy(ratings.at[0, 0], rat, loc_sem)
-    load.start()
+    loads = [
+        pltpu.make_async_copy(src, dst, loc_sem.at[k])
+        for k, (src, dst) in enumerate((
+            (uf_hbm, uf), (vf_hbm, vf), (cells_hbm, cells), (keep_hbm, keep),
+            (sends_hbm, sends), (unbr_hbm, unbr), (vnbr_hbm, vnbr), (ratings.at[0, 0], rat),
+        ))
+    ]
 
     barrier = pltpu.get_barrier_semaphore()
 
-    def greet_plane(d, _):
-        chip = lax.rem(p + d, CHIPS)
-        pl.semaphore_signal(barrier, inc=1, device_id=dev(chip, c), device_id_type=MESH)
+    def greet(device):
+        pl.semaphore_signal(barrier, inc=1, device_id=device, device_id_type=MESH)
+
+    def greet_y(d, _):
+        greet(dev(x * NY + lax.rem(y + d, NY), c))
         return 0
 
-    def greet_z(d, _):
-        pl.semaphore_signal(barrier, inc=1, device_id=(lax.rem(r + d, nrow), col), device_id_type=MESH)
+    def greet_x(d, _):
+        greet(dev(lax.rem(x + d, NX) * NY + y, c))
         return 0
 
-    lax.fori_loop(1, nrow, greet_z, 0)
-    lax.fori_loop(1, CHIPS, greet_plane, 0)
-    pl.semaphore_signal(barrier, inc=1, device_id=dev(p, other), device_id_type=MESH)
-
-    live = keep[0, 0]
-    for q in range(nrow):
-        live = live + sends[0, 0, q]
+    near_z = [3, nrow - 3, 2, nrow - 2, 1, nrow - 1]
+    lax.fori_loop(1, NY, greet_y, 0)
+    for d in near_z:
+        greet((lax.rem(r + d, nrow), col))
+    lax.fori_loop(1, NX, greet_x, 0)
+    greet(dev(p, other))
+    for copy in loads:
+        copy.start()
+    for copy in loads[:-1]:
+        copy.wait()
+
+    live = keep[...] + jnp.sum(sends[0], axis=1, keepdims=True)
     slot_at = lax.broadcasted_iota(jnp.int32, (128, slots), 1)
     cell_at = lax.broadcasted_iota(jnp.int32, (128, slots), 0)
     held = jnp.where((cells[0] == cell_at) & (slot_at < live), slot_at + 1, 0)
@@ -105,17 +122,14 @@
     ir[r] = jnp.zeros(ir.shape[1:], BF16)
     it[...] = jnp.zeros_like(it)
 
-    pl.semaphore_wait(barrier, nrow - 1 + CHIPS - 1 + 1)
-
-    def send_z(d, _):
-        to = lax.rem(r + d, nrow)
-        remote(vf.at[0], vg.at[r], z_send, z_recv, (to, col)).start()
-        return 0
-
-    def send_y(d, _):
+    pl.semaphore_wait(barrier, NY - 1 + NX - 1 + len(near_z) + 1)
+
+    def send_z(src, row, d):
+        remote(src, vg.at[row], z_send, z_recv.at[row], (lax.rem(r + d, nrow), col)).start()
+
+    def send_y(d):
         chip = x * NY + lax.rem(y + d, NY)
         remote(uf, ug.at[p, c], y_send, y_recv.at[y], dev(chip, c)).start()
-        return 0
 
     def spread_x(src, chip):
         def one(d, _):
@@ -128,8 +142,10 @@
     def to_partner(src, chip):
         remote(src, ug.at[chip, c], p_send, p_recv, dev(p, other)).start()
 
-    lax.fori_loop(1, NY, send_y, 0)
-    lax.fori_loop(1, nrow, send_z, 0)
+    for d in far_first(NY):
+        send_y(d)
+    for d in near_z:
+        send_z(vf.at[0], r, d)
     spread_x(uf, p)
     to_partner(uf, p)
 
@@ -140,6 +156,13 @@
         remote(piece, piece, y_send, y_recv.at[yy], dev(p, other)).wait_recv()
         spread_x(piece, chip)
         to_partner(piece, chip)
+    for d in [nrow - 3, 1, nrow - 1, 2, nrow - 2, 3]:
+        row = lax.rem(r + d, nrow)
+        remote(vg.at[row], vg.at[row], z_send, z_recv.at[row], dev(p, other)).wait_recv()
+        if d > nrow // 2:
+            send_z(vg.at[row], row, 3)
+        elif d < 3:
+            send_z(vg.at[row], row, nrow - 3)
     for d in [0] + ring_order(NY):
         yy = lax.rem(y + d, NY)
         for dx in ring_order(NX):
@@ -149,9 +172,10 @@
             to_partner(piece, chip)
 
     inv_copy.wait()
-    load.wait()
-    some = vg.at[pl.ds(0, nrow - 1)]
-    remote(some, some, z_send, z_recv, dev(p, other)).wait_recv()
+    loads[-1].wait()
+    for d in range(4, nrow - 3):
+        row = lax.rem(r + d, nrow)
+        remote(vg.at[row], vg.at[row], z_send, z_recv.at[row], dev(p, other)).wait_recv()
     some = ug.at[:, other]
     remote(some, some, p_send, p_recv, dev(p, other)).wait_recv()
 
@@ -211,12 +235,9 @@
     itf[...] = item_total
     ist[...] = item_total.astype(BF16)
 
-    def send_items(d, _):
+    for d in far_first(nrow):
         to = lax.rem(r + d, nrow)
         remote(ist.at[to], ir.at[r], ir_send, ir_recv, (to, col)).start()
-        return 0
-
-    lax.fori_loop(1, nrow, send_items, 0)
     for i in range(steps - lag, steps):
         pass_on(i)
 
@@ -273,16 +294,22 @@
             jax.ShapeDtypeStruct((1, irows, rank), F32),
         )
         vmem = pl.BlockSpec(memory_space=pltpu.VMEM)
-        smem = pl.BlockSpec(memory_space=pltpu.SMEM)
-        hbm = pl.BlockSpec(memory_space=pl.ANY)
+        hbm = pl.BlockSpec(memory_space=pltpu.HBM)
         dma = pltpu.SemaphoreType.DMA
         V = pltpu.VMEM
         outs = pl.pallas_call(
             functools.partial(kernel, nrow, 2),
             out_shape=outs_shape,
-            in_specs=[vmem, vmem, hbm, vmem, smem, smem, vmem, vmem],
+            in_specs=[hbm] * 8,
             out_specs=(vmem, vmem),
             scratch_shapes=[
+                V((urows, rank), BF16),
+                V((1, irows, rank), BF16),
+                V(cells.shape, jnp.int32),
+                V(keep.shape, jnp.int32),
+                V(sends.shape, jnp.int32),
+                V(unbr.shape[::-1], jnp.int32),
+                V((1, vnbr.shape[2], irows), jnp.int32),
                 V((CHIPS, NC, urows, rank), BF16),
                 V((nrow, irows, rank), BF16),
                 V((slots, tile, tile), BF16),
@@ -299,8 +326,8 @@
                 V((irows, nrow * irows), BF16),
                 V((8, 128), jnp.int32),
                 pltpu.SMEM((8, 128), jnp.int32),
-                dma((NY,)), dma((CHIPS,)), dma, dma, dma((CHIPS // 4,)), dma, dma,
-                dma, dma, dma, dma, dma, dma, dma, dma, dma,
+                dma((NY,)), dma((CHIPS,)), dma, dma((nrow,)), dma((CHIPS // 4,)), dma, dma,
+                dma, dma, dma, dma, dma, dma, dma, dma((8,)), dma,
             ],
             compiler_params=pltpu.CompilerParams(collective_id=0, has_side_effects=True),
         )(uf, vf, ratings, cells, keep, sends, unbr.T, jnp.swapaxes(vnbr, 1, 2))

time: 49.6 us -> 46.6 us (0.940)
  Pallas kernels: 48 us -> 45 us
    pallas_call x1, Pallas kernels: 46.6 us -> 43.6 us  [local(): pl.pallas_call(functools.partial(kernel, nrow, 2), out_shape=outs_shape,...]
where the time goes in v2:
time: 46.6 us; the launch traced here: 46.3 us
  Pallas kernels  45 us (97%)
  between operations  1.29 us (3%)
    pallas_call x1, Pallas kernels, local(): pl.pallas_call(functools.partial(kernel, nrow, 2), out_shape=outs_shape,...  43.6 us
    pallas_call x1, Pallas kernels, local(): pl.pallas_call(finish, out_shape=outs_shape, in_specs=[vmem, vmem], out_s...  1.4 us

profile of v2, /device:TPU:1, one launch (start us, length us, event | category | flops | bytes accessed | tf_op | source)
XLA Modules:
  0.0 46.3 jit_solution(10396199259178411265)
XLA Ops:
  1.3 43.6 %shard_map.95 = (f32[32,128]{1,0:T(8,128)}, f32[1,64,128]{2,1,0:T(8,128)}) custom-call(bf16[32,128]{1,0:T(8,128)(2,1)} %uf_hbm.1, bf16[1,64,128]{2,1,0:T(8,128)(2,1)} %vf_hbm.1, bf16[1,1,36,128,128]{4,3,2,1,0:T(8,128)(2,1)} %ratings.1, s32[1,1,36]{2,1,0:T(1,128)} %cells_hbm.1, s32[1,1]{1,0:T(1,128)S(6)} %copy.10.keep_hbm, s32[1,1,12]{2,1,0:T(1,128)} %sends_hbm.1, ...), custom_call_target="tpu_custom_call" | custom-call | tf_op jit(solution)/shard_map/pallas_call | solution.py:300
  44.9 1.4 %shard_map.96 = (f32[32,128]{1,0:T(8,128)}, f32[1,64,128]{2,1,0:T(8,128)}) custom-call(f32[32,128]{1,0:T(8,128)} %get-tuple-element.4.u_in, f32[1,64,128]{2,1,0:T(8,128)} %get-tuple-element.5.i_in), custom_call_target="tpu_custom_call" | custom-call | tf_op jit(solution)/shard_map/pallas_call | solution.py:334

commit v3 on v2

--- a/solution.py
+++ b/solution.py
@@ -114,13 +114,10 @@
     inv_copy = pltpu.make_async_copy(invv, invs, inv_sem)
     inv_copy.start()
 
-    au[...] = neighbour_counts(unbr[...], au.shape[1])
-    ai[...] = neighbour_counts(vnbr[0], ai.shape[1])
     ug[p, c] = uf[...]
     vg[r] = vf[0]
     ur[p] = jnp.zeros(ur.shape[1:], BF16)
     ir[r] = jnp.zeros(ir.shape[1:], BF16)
-    it[...] = jnp.zeros_like(it)
 
     pl.semaphore_wait(barrier, NY - 1 + NX - 1 + len(near_z) + 1)
 
@@ -181,66 +178,95 @@
 
     first = p // 4 + 1
 
+    def group(i):
+        return lax.rem(first + i, steps)
+
     def pass_on(i):
-        t = lax.rem(first + i + steps, steps)
-        four = pl.ds(t * 4, 4)
-        remote(pr.at[four], pr.at[four], pr_send, pr_recv.at[t], dev(p, other)).wait_recv()
-        us[four] = (ua[four, c] + pr[four]).astype(BF16)
+        remote(pr.at[i], pr.at[i], pr_send, pr_recv.at[i], dev(p, other)).wait_recv()
+        us[i] = (ua[i, :, c] + pr[i]).astype(BF16)
 
         def one(j, _):
-            chip = t * 4 + j
+            chip = group(i) * 4 + j
 
             @pl.when(chip != p)
             def _():
-                remote(us.at[chip], ur.at[p], ur_send, ur_recv, dev(chip, c)).start()
+                remote(us.at[i, j], ur.at[p], ur_send, ur_recv, dev(chip, c)).start()
 
             return 0
 
         lax.fori_loop(0, 4, one, 0)
 
-    def step(i, _):
-        t = lax.rem(first + i, steps)
-        four = pl.ds(t * 4, 4)
-        users = ug[four].reshape(2 * tile, -1)
-        for pair in range(vt // 2):
-            items = vg[pl.ds(pair * (2 * tile // irows), 2 * tile // irows)].reshape(2 * tile, -1)
-            product = lax.dot_general(
-                users, items, (((1,), (1,)), ((), ())), preferred_element_type=F32
+    span = 2 * tile // irows
+    own_pair = r // span
+    pairs = vt // 2
+    for turn in range(pairs):
+        last = turn == pairs - 1
+        pair = own_pair if last else lax.rem(own_pair + 1 + turn, pairs)
+        rows = pl.ds(pair * span, span)
+        items = vg[rows].reshape(2 * tile, -1)
+
+        def produce(j):
+            for i in (2 * j, 2 * j + 1):
+                t = group(i)
+                users = ug[pl.ds(t * 4, 4)].reshape(2 * tile, -1)
+                product = lax.dot_general(
+                    users, items, (((1,), (1,)), ((), ())), preferred_element_type=F32
+                )
+                for a in range(2):
+                    for b in range(2):
+                        slot = invs[0, (t * 2 + a) * vt + pair * 2 + b]
+                        weight = jnp.minimum(slot, 1).astype(F32)
+                        values = rat[jnp.clip(slot - 1, 0, slots - 1)].astype(F32)
+                        prefer = jnp.where(values > 0, 1.0, 0.0).astype(F32)
+                        part = product[a * tile : (a + 1) * tile, b * tile : (b + 1) * tile]
+                        error = (weight + (ALPHA * weight) * values) * (part - prefer)
+                        er[i, a * tile : (a + 1) * tile, b * tile : (b + 1) * tile] = error.astype(BF16)
+
+        def consume(j):
+            two = slice(2 * j, 2 * j + 2)
+            error = er[two].reshape(4 * tile, -1)
+            user_part = jnp.dot(error, items, preferred_element_type=F32)
+            user_part = user_part.reshape(2, 4, NC, urows, -1)
+            ua[two] = user_part if turn == 0 else ua[two] + user_part
+            users = jnp.concatenate(
+                [ug[pl.ds(group(i) * 4, 4)].reshape(2 * tile, -1) for i in (2 * j, 2 * j + 1)], axis=0
             )
-            for a in range(2):
-                for b in range(2):
-                    slot = invs[0, (t * 2 + a) * vt + pair * 2 + b]
-                    weight = jnp.minimum(slot, 1).astype(F32)
-                    values = rat[jnp.clip(slot - 1, 0, slots - 1)].astype(F32)
-                    prefer = jnp.where(values > 0, 1.0, 0.0).astype(F32)
-                    part = product[a * tile : (a + 1) * tile, b * tile : (b + 1) * tile]
-                    error = (weight + (ALPHA * weight) * values) * (part - prefer)
-                    er[a * tile : (a + 1) * tile, (pair * 2 + b) * tile : (pair * 2 + b + 1) * tile] = error.astype(BF16)
-        error = er[...]
-        items = vg[...].reshape(vt * tile, -1)
-        user_part = jnp.dot(error, items, preferred_element_type=F32)
-        ua[four] = user_part.reshape(4, NC, urows, -1)
-        it[...] += lax.dot_general(users, error, (((0,), (0,)), ((), ())), preferred_element_type=F32)
-        remote(ua.at[four, other], pr.at[four], pr_send, pr_recv.at[t], dev(p, other)).start()
-
-        @pl.when(i >= lag)
-        def _():
-            pass_on(i - lag)
-
-        return 0
-
-    lax.fori_loop(0, steps, step, 0)
-
-    item_total = jnp.transpose(it[...]).reshape(nrow, irows, -1)
-    itf[...] = item_total
-    ist[...] = item_total.astype(BF16)
-
-    for d in far_first(nrow):
-        to = lax.rem(r + d, nrow)
-        remote(ist.at[to], ir.at[r], ir_send, ir_recv, (to, col)).start()
-    for i in range(steps - lag, steps):
+            item_part = lax.dot_general(
+                users, error, (((0,), (0,)), ((), ())), preferred_element_type=F32
+            )
+            it[...] = item_part if j == 0 else it[...] + item_part
+
+        produce(0)
+        for j in range(steps // 2):
+            if j + 1 < steps // 2:
+                produce(j + 1)
+            consume(j)
+            if last:
+                for i in (2 * j, 2 * j + 1):
+                    remote(ua.at[i, :, other], pr.at[i], pr_send, pr_recv.at[i], dev(p, other)).start()
+                if j >= lag:
+                    pass_on(2 * (j - lag))
+                    pass_on(2 * (j - lag) + 1)
+
+        done = jnp.transpose(it[...]).reshape(span, irows, -1)
+        itf[rows] = done
+        ist[rows] = done.astype(BF16)
+
+        def send_item(j, _, pair=pair):
+            to = pair * span + j
+
+            @pl.when(to != r)
+            def _():
+                remote(ist.at[to], ir.at[r], ir_send, ir_recv, (to, col)).start()
+
+            return 0
+
+        lax.fori_loop(0, span, send_item, 0)
+    for i in range(steps - 2 * lag, steps):
         pass_on(i)
 
+    au[...] = neighbour_counts(unbr[...], au.shape[1])
+    ai[...] = neighbour_counts(vnbr[0], ai.shape[1])
     near = jnp.dot(au[...], ug[...].reshape(CHIPS * NC * urows, -1), preferred_element_type=F32)
     user_smooth = uf[...].astype(F32) - near / unbr.shape[0]
     near = jnp.dot(ai[...], vg[...].reshape(vt * tile, -1), preferred_element_type=F32)
@@ -248,7 +274,8 @@
 
     some = ur.at[pl.ds(0, CHIPS - 1)]
     remote(some, some, ur_send, ur_recv, dev(p, other)).wait_recv()
-    total = ua[p, c] + pr[p] + jnp.sum(ur[...].astype(F32), axis=0)
+    mine = lax.rem(p, 4)
+    total = ua[steps - 1, mine, c] + pr[steps - 1, mine] + jnp.sum(ur[...].astype(F32), axis=0)
     gu[...] = DATA_SCALE * total + SMOOTH * user_smooth
     some = ir.at[pl.ds(0, nrow - 1)]
     remote(some, some, ir_send, ir_recv, dev(p, other)).wait_recv()
@@ -263,7 +290,7 @@
     left(ug.at[:, c], p_send)
     left(vg.at[pl.ds(0, nrow - 1)], z_send)
     left(pr, pr_send)
-    left(us.at[pl.ds(0, CHIPS - 1)], ur_send)
+    left(ur.at[pl.ds(0, CHIPS - 1)], ur_send)
     left(ist.at[pl.ds(0, nrow - 1)], ir_send)
 
 
@@ -298,8 +325,8 @@
         dma = pltpu.SemaphoreType.DMA
         V = pltpu.VMEM
         outs = pl.pallas_call(
-            functools.partial(kernel, nrow, 2),
-            out_shape=outs_shape,
+            functools.partial(kernel, nrow, 1),
+            out_shape=(V((urows, rank), F32), V((1, irows, rank), F32)),
             in_specs=[hbm] * 8,
             out_specs=(vmem, vmem),
             scratch_shapes=[
@@ -313,12 +340,12 @@
                 V((CHIPS, NC, urows, rank), BF16),
                 V((nrow, irows, rank), BF16),
                 V((slots, tile, tile), BF16),
-                V((2 * tile, nrow * irows), BF16),
-                V((CHIPS, NC, urows, rank), F32),
-                V((rank, nrow * irows), F32),
+                V((CHIPS // 4, 2 * tile, 2 * tile), BF16),
+                V((CHIPS // 4, 4, NC, urows, rank), F32),
+                V((rank, 2 * tile), F32),
                 V((nrow, irows, rank), F32),
-                V((CHIPS, urows, rank), F32),
-                V((CHIPS, urows, rank), BF16),
+                V((CHIPS // 4, 4, urows, rank), F32),
+                V((CHIPS // 4, 4, urows, rank), BF16),
                 V((CHIPS, urows, rank), BF16),
                 V((nrow, irows, rank), BF16),
                 V((nrow, irows, rank), BF16),
@@ -336,7 +363,7 @@
             out_shape=outs_shape,
             in_specs=[vmem, vmem],
             out_specs=(vmem, vmem),
-        )(*outs)
+        )(*(pltpu.with_memory_space_constraint(o, pltpu.VMEM) for o in outs))
 
     return jax.shard_map(
         local,

time: 46.6 us -> 43 us (0.923)
  Pallas kernels: 45 us -> 41.5 us
    pallas_call x1, Pallas kernels: 43.6 us -> 40.9 us  [local(): pl.pallas_call(functools.partial(kernel, nrow, 1), out_shape=(V((urows, r...]
    pallas_call x1, Pallas kernels: 1.4 us -> 0.62 us  [local(): pl.pallas_call(finish, out_shape=outs_shape, in_specs=[vmem, vmem], out_s...]
where the time goes in v3:
time: 43 us; the launch traced here: 42.8 us
  Pallas kernels  41.5 us (97%)
  between operations  1.29 us (3%)
    pallas_call x1, Pallas kernels, local(): pl.pallas_call(functools.partial(kernel, nrow, 1), out_shape=(V((urows, r...  40.9 us

profile of v3, /device:TPU:1, one launch (start us, length us, event | category | flops | bytes accessed | tf_op | source)
XLA Modules:
  0.0 42.8 jit_solution(12636529982025765459)
XLA Ops:
  1.3 40.9 %shard_map.95 = (f32[32,128]{1,0:T(8,128)S(1)}, f32[1,64,128]{2,1,0:T(8,128)S(1)}) custom-call(bf16[32,128]{1,0:T(8,128)(2,1)} %uf_hbm.1, bf16[1,64,128]{2,1,0:T(8,128)(2,1)} %vf_hbm.1, bf16[1,1,36,128,128]{4,3,2,1,0:T(8,128)(2,1)} %ratings.1, s32[1,1,36]{2,1,0:T(1,128)} %cells_hbm.1, s32[1,1]{1,0:T(1,128)S(6)} %copy.10.keep_hbm, s32[1,1,12]{2,1,0:T(1,128)} %sends_hbm.1, ...), custom_call_target="tpu_custom_call" | custom-call | tf_op jit(solution)/shard_map/pallas_call | solution.py:327
  42.2 0.6 %shard_map.96 = (f32[32,128]{1,0:T(8,128)}, f32[1,64,128]{2,1,0:T(8,128)}) custom-call(f32[32,128]{1,0:T(8,128)S(1)} %get-tuple-element.4.u_in, f32[1,64,128]{2,1,0:T(8,128)S(1)} %get-tuple-element.5.i_in), custom_call_target="tpu_custom_call" | custom-call | tf_op jit(solution)/shard_map/pallas_call | solution.py:361

commit v4 on v3

--- a/solution.py
+++ b/solution.py
@@ -199,11 +199,11 @@
     span = 2 * tile // irows
     own_pair = r // span
     pairs = vt // 2
-    for turn in range(pairs):
-        last = turn == pairs - 1
-        pair = own_pair if last else lax.rem(own_pair + 1 + turn, pairs)
-        rows = pl.ds(pair * span, span)
-        items = vg[rows].reshape(2 * tile, -1)
+    for turn in range(2):
+        last = turn == 1
+        held = [own_pair] if last else [lax.rem(own_pair + k, pairs) for k in range(1, pairs)]
+        width = 2 * tile * len(held)
+        items = jnp.concatenate([vg[pl.ds(pair * span, span)].reshape(2 * tile, -1) for pair in held], axis=0)
 
         def produce(j):
             for i in (2 * j, 2 * j + 1):
@@ -213,8 +213,8 @@
                     users, items, (((1,), (1,)), ((), ())), preferred_element_type=F32
                 )
                 for a in range(2):
-                    for b in range(2):
-                        slot = invs[0, (t * 2 + a) * vt + pair * 2 + b]
+                    for b in range(2 * len(held)):
+                        slot = invs[0, (t * 2 + a) * vt + held[b // 2] * 2 + b % 2]
                         weight = jnp.minimum(slot, 1).astype(F32)
                         values = rat[jnp.clip(slot - 1, 0, slots - 1)].astype(F32)
                         prefer = jnp.where(values > 0, 1.0, 0.0).astype(F32)
@@ -224,7 +224,7 @@
 
         def consume(j):
             two = slice(2 * j, 2 * j + 2)
-            error = er[two].reshape(4 * tile, -1)
+            error = er[two, :, :width].reshape(4 * tile, width)
             user_part = jnp.dot(error, items, preferred_element_type=F32)
             user_part = user_part.reshape(2, 4, NC, urows, -1)
             ua[two] = user_part if turn == 0 else ua[two] + user_part
@@ -234,7 +234,7 @@
             item_part = lax.dot_general(
                 users, error, (((0,), (0,)), ((), ())), preferred_element_type=F32
             )
-            it[...] = item_part if j == 0 else it[...] + item_part
+            it[:, :width] = item_part if j == 0 else it[:, :width] + item_part
 
         produce(0)
         for j in range(steps // 2):
@@ -248,20 +248,22 @@
                     pass_on(2 * (j - lag))
                     pass_on(2 * (j - lag) + 1)
 
-        done = jnp.transpose(it[...]).reshape(span, irows, -1)
-        itf[rows] = done
-        ist[rows] = done.astype(BF16)
-
-        def send_item(j, _, pair=pair):
+        done = jnp.transpose(it[:, :width]).reshape(len(held), span, irows, -1)
+        for k, pair in enumerate(held):
+            itf[pl.ds(pair * span, span)] = done[k]
+            ist[pl.ds(pair * span, span)] = done[k].astype(BF16)
+
+        def send_item(j, pair):
             to = pair * span + j
 
             @pl.when(to != r)
             def _():
                 remote(ist.at[to], ir.at[r], ir_send, ir_recv, (to, col)).start()
 
-            return 0
-
-        lax.fori_loop(0, span, send_item, 0)
+            return pair
+
+        for pair in held:
+            lax.fori_loop(0, span, send_item, pair)
     for i in range(steps - 2 * lag, steps):
         pass_on(i)
 
@@ -340,9 +342,9 @@
                 V((CHIPS, NC, urows, rank), BF16),
                 V((nrow, irows, rank), BF16),
                 V((slots, tile, tile), BF16),
-                V((CHIPS // 4, 2 * tile, 2 * tile), BF16),
+                V((CHIPS // 4, 2 * tile, nrow * irows - 2 * tile), BF16),
                 V((CHIPS // 4, 4, NC, urows, rank), F32),
-                V((rank, 2 * tile), F32),
+                V((rank, nrow * irows - 2 * tile), F32),
                 V((nrow, irows, rank), F32),
                 V((CHIPS // 4, 4, urows, rank), F32),
                 V((CHIPS // 4, 4, urows, rank), BF16),

time: 43 us -> 43.8 us (1.019)
  Pallas kernels: 41.5 us -> 42.3 us
    pallas_call x1, Pallas kernels: 40.9 us -> 41.7 us  [local(): pl.pallas_call(functools.partial(kernel, nrow, 1), out_shape=(V((urows, r...]
where the time goes in v4:
time: 43.8 us; the launch traced here: 43.6 us
  Pallas kernels  42.3 us (97%)
  between operations  1.29 us (3%)
    pallas_call x1, Pallas kernels, local(): pl.pallas_call(functools.partial(kernel, nrow, 1), out_shape=(V((urows, r...  41.7 us

profile of v4, /device:TPU:1, one launch (start us, length us, event | category | flops | bytes accessed | tf_op | source)
XLA Modules:
  0.0 43.6 jit_solution(15254514073131903128)
XLA Ops:
  1.3 41.7 %shard_map.95 = (f32[32,128]{1,0:T(8,128)S(1)}, f32[1,64,128]{2,1,0:T(8,128)S(1)}) custom-call(bf16[32,128]{1,0:T(8,128)(2,1)} %uf_hbm.1, bf16[1,64,128]{2,1,0:T(8,128)(2,1)} %vf_hbm.1, bf16[1,1,36,128,128]{4,3,2,1,0:T(8,128)(2,1)} %ratings.1, s32[1,1,36]{2,1,0:T(1,128)} %cells_hbm.1, s32[1,1]{1,0:T(1,128)S(6)} %copy.10.keep_hbm, s32[1,1,12]{2,1,0:T(1,128)} %sends_hbm.1, ...), custom_call_target="tpu_custom_call" | custom-call | tf_op jit(solution)/shard_map/pallas_call | solution.py:329
  43.0 0.6 %shard_map.96 = (f32[32,128]{1,0:T(8,128)}, f32[1,64,128]{2,1,0:T(8,128)}) custom-call(f32[32,128]{1,0:T(8,128)S(1)} %get-tuple-element.4.u_in, f32[1,64,128]{2,1,0:T(8,128)S(1)} %get-tuple-element.5.i_in), custom_call_target="tpu_custom_call" | custom-call | tf_op jit(solution)/shard_map/pallas_call | solution.py:363

commit v5 on v3

--- a/solution.py
+++ b/solution.py
@@ -137,7 +137,7 @@
         lax.fori_loop(1, NX, one, 0)
 
     def to_partner(src, chip):
-        remote(src, ug.at[chip, c], p_send, p_recv, dev(p, other)).start()
+        remote(src, ug.at[chip, c], p_send, p_recv.at[chip // NY], dev(p, other)).start()
 
     for d in far_first(NY):
         send_y(d)
@@ -170,11 +170,15 @@
 
     inv_copy.wait()
     loads[-1].wait()
-    for d in range(4, nrow - 3):
-        row = lax.rem(r + d, nrow)
-        remote(vg.at[row], vg.at[row], z_send, z_recv.at[row], dev(p, other)).wait_recv()
-    some = ug.at[:, other]
-    remote(some, some, p_send, p_recv, dev(p, other)).wait_recv()
+
+    def far_items():
+        for d in range(4, nrow - 3):
+            row = lax.rem(r + d, nrow)
+            remote(vg.at[row], vg.at[row], z_send, z_recv.at[row], dev(p, other)).wait_recv()
+
+    def partner_users(xx):
+        some = ug.at[pl.ds(xx * NY, NY), other]
+        remote(some, some, p_send, p_recv.at[xx], dev(p, other)).wait_recv()
 
     first = p // 4 + 1
 
@@ -201,13 +205,20 @@
     pairs = vt // 2
     for turn in range(pairs):
         last = turn == pairs - 1
-        pair = own_pair if last else lax.rem(own_pair + 1 + turn, pairs)
+        pair = lax.rem(own_pair + 1 + turn, pairs)
+        if turn == 0:
+            far_items()
         rows = pl.ds(pair * span, span)
         items = vg[rows].reshape(2 * tile, -1)
 
+        def visited(j, turn=turn):
+            if turn:
+                return group(2 * j), group(2 * j + 1)
+            xx = lax.rem(x + ([0] + ring_order(NX))[j], NX)
+            return 2 * xx, 2 * xx + 1
+
         def produce(j):
-            for i in (2 * j, 2 * j + 1):
-                t = group(i)
+            for i, t in zip((2 * j, 2 * j + 1), visited(j)):
                 users = ug[pl.ds(t * 4, 4)].reshape(2 * tile, -1)
                 product = lax.dot_general(
                     users, items, (((1,), (1,)), ((), ())), preferred_element_type=F32
@@ -227,19 +238,26 @@
             error = er[two].reshape(4 * tile, -1)
             user_part = jnp.dot(error, items, preferred_element_type=F32)
             user_part = user_part.reshape(2, 4, NC, urows, -1)
-            ua[two] = user_part if turn == 0 else ua[two] + user_part
+            if turn:
+                ua[two] = ua[two] + user_part
+            else:
+                for k, t in enumerate(visited(j)):
+                    ua[lax.rem(t - first + 2 * steps, steps)] = user_part[k]
             users = jnp.concatenate(
-                [ug[pl.ds(group(i) * 4, 4)].reshape(2 * tile, -1) for i in (2 * j, 2 * j + 1)], axis=0
+                [ug[pl.ds(t * 4, 4)].reshape(2 * tile, -1) for t in visited(j)], axis=0
             )
             item_part = lax.dot_general(
                 users, error, (((0,), (0,)), ((), ())), preferred_element_type=F32
             )
             it[...] = item_part if j == 0 else it[...] + item_part
 
-        produce(0)
-        for j in range(steps // 2):
+        for j in range(-1, steps // 2):
             if j + 1 < steps // 2:
+                if turn == 0:
+                    partner_users(visited(j + 1)[0] // 2)
                 produce(j + 1)
+            if j < 0:
+                continue
             consume(j)
             if last:
                 for i in (2 * j, 2 * j + 1):
@@ -353,7 +371,7 @@
                 V((irows, nrow * irows), BF16),
                 V((8, 128), jnp.int32),
                 pltpu.SMEM((8, 128), jnp.int32),
-                dma((NY,)), dma((CHIPS,)), dma, dma((nrow,)), dma((CHIPS // 4,)), dma, dma,
+                dma((NY,)), dma((CHIPS,)), dma((NX,)), dma((nrow,)), dma((CHIPS // 4,)), dma, dma,
                 dma, dma, dma, dma, dma, dma, dma, dma((8,)), dma,
             ],
             compiler_params=pltpu.CompilerParams(collective_id=0, has_side_effects=True),

time: 43 us -> 43 us (level)
  no operation moved by 1% of the time
where the time goes in v5:
time: 43 us; the launch traced here: 42.8 us
  Pallas kernels  41.6 us (97%)
  between operations  1.29 us (3%)
    pallas_call x1, Pallas kernels, local(): pl.pallas_call(functools.partial(kernel, nrow, 1), out_shape=(V((urows, r...  40.9 us

profile of v5, /device:TPU:1, one launch (start us, length us, event | category | flops | bytes accessed | tf_op | source)
XLA Modules:
  0.0 42.8 jit_solution(14172407500600474351)
XLA Ops:
  1.3 40.9 %shard_map.95 = (f32[32,128]{1,0:T(8,128)S(1)}, f32[1,64,128]{2,1,0:T(8,128)S(1)}) custom-call(bf16[32,128]{1,0:T(8,128)(2,1)} %uf_hbm.1, bf16[1,64,128]{2,1,0:T(8,128)(2,1)} %vf_hbm.1, bf16[1,1,36,128,128]{4,3,2,1,0:T(8,128)(2,1)} %ratings.1, s32[1,1,36]{2,1,0:T(1,128)} %cells_hbm.1, s32[1,1]{1,0:T(1,128)S(6)} %copy.10.keep_hbm, s32[1,1,12]{2,1,0:T(1,128)} %sends_hbm.1, ...), custom_call_target="tpu_custom_call" | custom-call | tf_op jit(solution)/shard_map/pallas_call | solution.py:345
  42.2 0.6 %shard_map.96 = (f32[32,128]{1,0:T(8,128)}, f32[1,64,128]{2,1,0:T(8,128)}) custom-call(f32[32,128]{1,0:T(8,128)S(1)} %get-tuple-element.4.u_in, f32[1,64,128]{2,1,0:T(8,128)S(1)} %get-tuple-element.5.i_in), custom_call_target="tpu_custom_call" | custom-call | tf_op jit(solution)/shard_map/pallas_call | solution.py:379
